TPU v7x, 256 devices: a whole 4x4x8 slice. The times are simulated.
256 devices in a mesh: req: 16 (over z_hi, y, core), tp: 16 (over z_lo, x).
Axes of the slice: x: 4, y: 4, z: 8 (z_hi: 2, z_lo: 4; z = z_hi * 4 + z_lo), core: 2. Of those that a mesh axis runs over, the one named last changes fastest.
Arguments:
- queries: bfloat16 [64, 32, 4096], P('req'), may hold values from -128 to 128
- cache_keys: bfloat16 [64, 4096, 512], P('req', 'tp'), may hold values from -4 to 4
- cache_values: bfloat16 [64, 4096, 512], P('req', 'tp'), may hold values from -5 to 5
- tree_keys: bfloat16 [64, 32, 512], P('req', 'tp'), may hold values from -5 to 5
- tree_values: bfloat16 [64, 32, 512], P('req', 'tp'), may hold values from -5 to 5
- parents: int32 [64, 32], P('req'), may hold values from -1 to 30, as said below
- lengths: int32 [64], P('req'), may hold values from 2 to 4096
- accepted_leaf: int32 [64], P('req'), may hold values from 0 to 31
- residual: bfloat16 [64, 32, 8192], P('req', None, 'tp'), may hold values from -12 to 12
- norm_gain: float32 [8192], replicated, may hold values from 0.5 to 4
- out_weight: bfloat16 [4096, 8192], P('tp'), may hold values from -0.09375 to 0.09375
- prev_feature: bfloat16 [64, 8192], P('req'), may hold values from -5 to 5
- draft_weight: bfloat16 [8192, 8192], P('req', 'tp'), may hold values from -0.0625 to 0.0625
- first_moment: float32 [8192, 8192], P('req', 'tp'), may hold values from -5 to 5
- second_moment: float32 [8192, 8192], P('req', 'tp'), may hold values from 0.25 to 4
Outputs:
- features: bfloat16 [64, 32, 8192], P('req', None, 'tp')
- new_weight: bfloat16 [8192, 8192], P('req', 'tp')
- new_first: float32 [8192, 8192], P('req', 'tp')
- new_second: float32 [8192, 8192], P('req', 'tp')
- draft_loss: float32 [], replicated
Inputs may be any that keep to these rules, and one draw needn't show every extreme that they name: parents[r, 0] = -1; for i of 1 or more, parents[r, i] lies in 0 to i - 1; node 31 is a child of node 30.
All inputs are finite; a program needn't handle non-finite values.
Results may differ from a plain program's by a relative error of at most 0.014.
Values may be sent and summed in bfloat16 or wider, within the bound.
No kernel may reach another device: no remote copies, remote signals or barrier semaphores. Data moves between devices by JAX's collectives and lax.ppermute only.
A program may use at most 128 MiB of HBM per device.

v0:
```python
import math
import jax
import jax.numpy as jnp
from jax import lax
from jax.sharding import PartitionSpec as P

HEADS = 32
KV_HEADS = 4
HEAD = 128
NODES = 32
CACHE = 4096
NEG_FILL = -1e30
NORM_EPSILON = 1e-06
BETA_ONE = 0.9
BETA_TWO = 0.95
CORRECT_ONE = 1.0 - 0.9**10
CORRECT_TWO = 1.0 - 0.95**10
LEARN_RATE = 0.001


def closure(parents):
    node_count = parents.shape[-1]
    onehot = (parents[:, :, None] == jnp.arange(node_count, dtype=jnp.int32)[None, None, :]).astype(
        jnp.float32
    )
    reach_map = jnp.eye(node_count, dtype=jnp.float32)[None] + onehot
    for repeat in range(node_count.bit_length()):
        reach_map = jnp.minimum(
            jnp.einsum("rij,rjk->rik", reach_map, reach_map, precision=lax.Precision.HIGHEST), 1.0
        )
    return reach_map


def body(
    queries,
    cache_keys,
    cache_values,
    tree_keys,
    tree_values,
    parents,
    lengths,
    accepted_leaf,
    residual,
    norm_gain,
    out_weight,
    prev_feature,
    draft_weight,
    first_moment,
    second_moment,
):
    full_residual = lax.all_gather(residual, "tp", axis=2, tiled=True)
    requests = queries.shape[0]
    row_count = requests * NODES
    groups = HEADS // KV_HEADS
    score_scale = 1.0 / math.sqrt(HEAD)
    tp_rank = lax.axis_index("tp")
    cache_span = cache_keys.shape[1]
    tree_span = tree_keys.shape[1]
    reach_map = closure(parents)
    query_view = queries.reshape(requests, NODES, KV_HEADS, groups, HEAD)
    cache_view = cache_keys.reshape(requests, cache_span, KV_HEADS, HEAD)
    tree_view = tree_keys.reshape(requests, tree_span, KV_HEADS, HEAD)
    cache_scores = (
        jnp.einsum("rnkgd,rckd->rkgnc", query_view, cache_view, preferred_element_type=jnp.float32)
        * score_scale
    )
    tree_scores = (
        jnp.einsum("rnkgd,rjkd->rkgnj", query_view, tree_view, preferred_element_type=jnp.float32)
        * score_scale
    )
    positions = tp_rank * cache_span + jnp.arange(cache_span, dtype=jnp.int32)
    cache_live = (positions[None, :] < lengths[:, None])[:, None, None, None, :]
    visible = lax.dynamic_slice_in_dim(reach_map, tp_rank * tree_span, tree_span, 2)
    tree_live = (visible > 0.5)[:, None, None, :, :]
    cache_scores = jnp.where(cache_live, cache_scores, NEG_FILL)
    tree_scores = jnp.where(tree_live, tree_scores, NEG_FILL)
    local_top = jnp.maximum(jnp.max(cache_scores, axis=-1), jnp.max(tree_scores, axis=-1))
    row_top = lax.pmax(local_top, "tp")
    cache_probs = jnp.where(cache_live, jnp.exp(cache_scores - row_top[..., None]), 0.0).astype(
        jnp.bfloat16
    )
    tree_probs = jnp.where(tree_live, jnp.exp(tree_scores - row_top[..., None]), 0.0).astype(
        jnp.bfloat16
    )
    totals = jnp.sum(cache_probs, axis=-1, dtype=jnp.float32) + jnp.sum(
        tree_probs, axis=-1, dtype=jnp.float32
    )
    value_view = cache_values.reshape(requests, cache_span, KV_HEADS, HEAD)
    tree_value_view = tree_values.reshape(requests, tree_span, KV_HEADS, HEAD)
    weighted = jnp.einsum(
        "rkgnc,rckd->rnkgd", cache_probs, value_view, preferred_element_type=jnp.float32
    )
    weighted = weighted + jnp.einsum(
        "rkgnj,rjkd->rnkgd", tree_probs, tree_value_view, preferred_element_type=jnp.float32
    )
    weighted = weighted.reshape(row_count, HEADS * HEAD)
    totals = jnp.transpose(totals, (0, 3, 1, 2)).reshape(row_count, HEADS)
    head_sums, head_totals = (
        lax.psum_scatter(weighted, "tp", scatter_dimension=1, tiled=True),
        lax.psum_scatter(totals, "tp", scatter_dimension=1, tiled=True),
    )
    own_heads = head_totals.shape[1]
    attended = (head_sums.reshape(row_count, own_heads, HEAD) / head_totals[:, :, None]).astype(
        jnp.bfloat16
    )
    partial_value = jnp.dot(
        attended.reshape(row_count, own_heads * HEAD),
        out_weight,
        preferred_element_type=jnp.float32,
    )
    partial_value = lax.optimization_barrier(partial_value.astype(jnp.bfloat16)).astype(jnp.float32)
    model_width = partial_value.shape[1]
    block_width = model_width // lax.axis_size("tp")
    summed = lax.psum(partial_value.astype(jnp.bfloat16), "tp").astype(jnp.float32)
    mixed = full_residual.reshape(row_count, model_width).astype(jnp.float32) + summed
    mean_sq = jnp.mean(mixed * mixed, axis=1, keepdims=True)
    features = (mixed * lax.rsqrt(mean_sq + NORM_EPSILON) * norm_gain[None, :]).astype(jnp.bfloat16)
    own_block = lax.dynamic_slice_in_dim(features, tp_rank * block_width, block_width, 1)
    feature_table = jnp.concatenate(
        [prev_feature[:, None, :], features.reshape(requests, NODES, model_width)], axis=1
    )
    inputs = jnp.take_along_axis(feature_table, (parents + 1)[:, :, None], axis=1).reshape(
        row_count, model_width
    )
    leaf_hot = (accepted_leaf[:, None] == jnp.arange(NODES, dtype=jnp.int32)[None, :]).astype(
        jnp.float32
    )
    accepted = jnp.einsum("rn,rnj->rj", leaf_hot, reach_map, precision=lax.Precision.HIGHEST)
    fill_share = 0.5 + lengths.astype(jnp.float32) / CACHE
    weights = ((1.0 + 3.0 * accepted) * fill_share[:, None]).reshape(row_count, 1)
    columns = inputs
    predicted = jnp.dot(
        columns,
        lax.all_gather(draft_weight, "req", axis=0, tiled=True),
        preferred_element_type=jnp.float32,
    )
    pred_error = predicted - own_block.astype(jnp.float32)
    scaled_err = (weights * pred_error).astype(jnp.bfloat16)
    columns = inputs
    gradient = lax.psum_scatter(
        lax.dot_general(
            columns, scaled_err, (((0,), (0,)), ((), ())), preferred_element_type=jnp.float32
        ),
        "req",
        scatter_dimension=0,
        tiled=True,
    )
    square_total, error_total = lax.psum(
        (jnp.sum(gradient * gradient), jnp.sum(weights * pred_error * pred_error)), ("req", "tp")
    )
    draft_loss = 0.5 * error_total / (row_count * lax.axis_size("req") * model_width)
    grad_norm = jnp.sqrt(square_total) + 1e-06
    clip_factor = jnp.minimum(1.0, model_width / grad_norm)
    clipped = gradient * clip_factor
    new_first = BETA_ONE * first_moment + (1.0 - BETA_ONE) * clipped
    new_second = BETA_TWO * second_moment + (1.0 - BETA_TWO) * clipped * clipped
    direction = new_first / CORRECT_ONE / (jnp.sqrt(new_second / CORRECT_TWO) + 1e-08)
    new_weight = (draft_weight.astype(jnp.float32) - LEARN_RATE * direction).astype(jnp.bfloat16)
    return (
        own_block.reshape(requests, NODES, block_width),
        new_weight,
        new_first,
        new_second,
        draft_loss,
    )


def solution(mesh):
    placed = (
        P("req", None, None),
        P("req", "tp", None),
        P("req", "tp", None),
        P("req", "tp", None),
        P("req", "tp", None),
        P("req", None),
        P("req"),
        P("req"),
        P("req", None, "tp"),
        P(),
        P("tp", None),
        P("req", None),
        P("req", "tp"),
        P("req", "tp"),
        P("req", "tp"),
    )
    return jax.shard_map(
        body,
        mesh=mesh,
        in_specs=placed,
        out_specs=(P("req", None, "tp"), P("req", "tp"), P("req", "tp"), P("req", "tp"), P()),
        check_vma=False,
    )
```

profile of v0, /device:TPU:1, one launch (start us, length us, event | category | flops | bytes accessed | tf_op | source)
XLA Modules:
  0.0 868.4 jit_solution(2874297902461404456)
XLA Ops:
  7.3 1.1 convolution_minimum_fusion.4
  10.4 1.4 copy.89
  11.8 1.1 reshape.107
  13.3 1.5 fusion.38
  14.8 4.1 bitcast_reduce_fusion
  19.0 67.8 %pmax.7 = f32[4,4,8,32]{3,2,1,0:T(8,128)S(1)} all-reduce(f32[4,4,8,32]{3,2,1,0:T(8,128)S(1)} %max.5), channel_id=1, replica_groups=mesh['req'=16,'tp'=16] {'tp'}, use_global_device_ids=true, to_apply=%region_2.3 | all-reduce | flops 4096 | bytes 32768 | tf_op jit(solution)/shard_map/pmax | solution.py:78
  87.0 3.0 fusion.6
  90.0 0.5 add_bitcast_fusion
  90.5 1.2 copy.74
  91.7 1.5 reshape.112
  93.3 0.7 all-gather.3.cloned.1.call-update
  94.1 3.1 convert_reduce_fusion
  97.4 0.6 dynamic-slice
  98.6 61.0 %all-reduce = f32[128,32]{0,1:T(8,128)S(1)} all-reduce(f32[128,32]{0,1:T(8,128)S(1)} %reshape.113), channel_id=3, replica_groups=mesh['req'=16,'tp'=16] {'tp'}, use_global_device_ids=true, to_apply=%region_6.7.clone | all-reduce | flops 4096 | bytes 32768
  159.7 23.9 %reduce-scatter.3.cloned.1.call-done = f32[128,256]{1,0:T(8,128)} async-done(((f32[128,4096]{1,0:T(8,128)}), f32[128,256]{1,0:T(8,128)}) %reduce-scatter.3.cloned.1.call-update) | async-done | bytes 131088 | tf_op jit(solution)/shard_map/reduce_scatter | solution.py:99
  183.9 4.3 convolution_convert_fusion
  188.3 0.5 all-gather.5.cloned.1.call-update
  189.7 75.2 %all-gather.3.cloned.1.call-done = bf16[4,32,8192]{2,1,0:T(8,128)(2,1)} async-done(((bf16[4,32,512]{2,1,0:T(8,128)(2,1)}), bf16[4,32,8192]{2,1,0:T(8,128)(2,1)}) %all-gather.3.cloned.1.call-update) | async-done | bytes 2097168 | tf_op jit(solution)/shard_map/all_gather | solution.py:51
  264.8 168.2 %all-reduce.4.cloned.1.call-done = bf16[128,8192]{1,0:T(8,128)(2,1)} async-done(((bf16[128,8192]{1,0:T(8,128)(2,1)}), bf16[128,8192]{1,0:T(8,128)(2,1)}) %all-reduce.4.cloned.1.call-update) | async-done | bytes 2097168 | tf_op jit(solution)/shard_map/psum | solution.py:114
  433.0 3.1 multiply_reduce_fusion
  436.2 1.0 multiply_convert_fusion
  437.2 1.6 copy.77
  438.9 1.4 pad_maximum_fusion
  440.3 8.3 gather_fusion
  448.5 0.9 constant_dynamic-slice_fusion.1
  449.5 103.7 %all-gather.5.cloned.1.call-done = bf16[8192,512]{1,0:T(8,128)(2,1)} async-done(((bf16[512,512]{1,0:T(8,128)(2,1)}), bf16[8192,512]{1,0:T(8,128)(2,1)}) %all-gather.5.cloned.1.call-update) | async-done | bytes 8388624 | tf_op jit(solution)/shard_map/all_gather | solution.py:134
  553.2 6.2 fusion.13
  559.4 8.2 fusion.12
  567.6 210.0 %reduce-scatter.5.cloned.1.call-done = f32[512,512]{1,0:T(8,128)} async-done(((f32[8192,512]{1,0:T(8,128)}), f32[512,512]{1,0:T(8,128)}) %reduce-scatter.5.cloned.1.call-update) | async-done | bytes 1048592 | tf_op jit(solution)/shard_map/reduce_scatter | solution.py:140
  777.6 2.1 multiply_reduce_fusion.1
  779.7 76.2 %all-reduce.1 = (f32[]{:T(128)}, f32[]{:T(128)}) all-reduce(f32[]{:T(128)} %multiply_reduce_fusion.1, f32[]{:T(128)} %get-tuple-element.16), channel_id=1, replica_groups=mesh['req'=16,'tp'=16] {'req','tp'}, use_global_device_ids=true, to_apply=%region_11.12 | all-reduce | flops 2 | bytes 16 | tf_op jit(solution)/shard_map/psum | solution.py:148
  857.3 3.4 subtract_convert_fusion
  (81 shorter events, 4.1 us)
Async XLA Ops:
  7.2 82.8 %copy-start = (bf16[4,2,512]{2,1,0:T(2,128)(2,1)S(1)}, bf16[4,2,512]{2,1,0:T(2,128)(2,1)}, u32[]{:S(2)}) copy-start(bf16[4,2,512]{2,1,0:T(2,128)(2,1)} %param.19) | copy-start | bytes 24580
  7.2 4.7 copy-start.9
  7.2 5.8 copy-start.10
  7.2 6.0 copy-start.15
  7.2 6.1 copy-start.16
  7.2 176.4 %reduce-scatter.3.cloned.1.call-start = ((), (), s32[]{:S(2)}) async-start(), calls=%async_computation.3 | async-start | bytes 2228224 | tf_op jit(solution)/shard_map/reduce_scatter | solution.py:99
  93.2 4.2 copy-start.18
  93.3 171.5 %all-gather.3.cloned.1.call-start = ((), (), s32[]{:S(2)}) async-start(), calls=%async_computation.2 | async-start | bytes 2228224 | tf_op jit(solution)/shard_map/all_gather | solution.py:51
  94.0 338.9 %all-reduce.4.cloned.1.call-start = ((), (), s32[]{:S(2)}) async-start(), calls=%async_computation.4 | async-start | bytes 4194304 | tf_op jit(solution)/shard_map/psum | solution.py:114
  183.9 5.2 copy-start.14
  183.9 5.4 copy-start.17
  188.2 247.9 %copy-start.13 = (f32[8192]{0:T(1024)S(1)}, f32[8192]{0:T(1024)}, u32[]{:S(2)}) copy-start(f32[8192]{0:T(1024)} %param.24) | copy-start | bytes 98308
  188.2 365.0 %all-gather.5.cloned.1.call-start = ((), (), s32[]{:S(2)}) async-start(), calls=%async_computation.5 | async-start | bytes 8912896 | tf_op jit(solution)/shard_map/all_gather | solution.py:134
  188.8 588.8 %reduce-scatter.5.cloned.1.call-start = ((), (), s32[]{:S(2)}) async-start(), calls=%async_computation.6 | async-start | bytes 17825792 | tf_op jit(solution)/shard_map/reduce_scatter | solution.py:140
  264.8 171.3 %copy-start.4 = (bf16[4,32,8192]{2,1,0:T(8,128)(2,1)S(1)}, bf16[4,32,8192]{2,1,0:T(8,128)(2,1)}, u32[]{:S(2)}) copy-start(bf16[4,32,8192]{2,1,0:T(8,128)(2,1)} %all-gather.3.cloned.1.call-done) | copy-start | bytes 6291460
  433.0 3.2 copy-start.5
  436.1 2.7 copy-start.12
  437.2 1.6 copy-start.3
  449.5 109.9 %copy-start.11 = (bf16[128,512]{1,0:T(8,128)(2,1)}, bf16[128,512]{1,0:T(8,128)(2,1)S(1)}, u32[]{:S(2)}) copy-start(bf16[128,512]{1,0:T(8,128)(2,1)S(1)} %constant_dynamic-slice_fusion.1) | copy-start | bytes 393220
  449.5 109.9 %copy-start.2 = (bf16[128,8192]{1,0:T(8,128)(2,1)S(1)}, bf16[128,8192]{1,0:T(8,128)(2,1)}, u32[]{:S(2)}) copy-start(bf16[128,8192]{1,0:T(8,128)(2,1)} %gather_fusion) | copy-start | bytes 6291460
  567.6 289.7 %copy-start.6 = (bf16[512,512]{1,0:T(8,128)(2,1)S(1)}, bf16[512,512]{1,0:T(8,128)(2,1)}, u32[]{:S(2)}) copy-start(bf16[512,512]{1,0:T(8,128)(2,1)} %param.27) | copy-start | bytes 1572868
  567.6 289.7 %copy-start.7 = (f32[512,512]{1,0:T(8,128)S(1)}, f32[512,512]{1,0:T(8,128)}, u32[]{:S(2)}) copy-start(f32[512,512]{1,0:T(8,128)} %param.28) | copy-start | bytes 3145732
  567.6 289.7 %copy-start.8 = (f32[512,512]{1,0:T(8,128)S(1)}, f32[512,512]{1,0:T(8,128)}, u32[]{:S(2)}) copy-start(f32[512,512]{1,0:T(8,128)} %param.29) | copy-start | bytes 3145732
  567.6 293.1 %copy-start.1 = (bf16[4,2,512]{2,1,0:T(2,128)(2,1)S(1)}, bf16[4,2,512]{2,1,0:T(2,128)(2,1)}, u32[]{:S(2)}) copy-start(bf16[4,2,512]{2,1,0:T(2,128)(2,1)} %param.19) | copy-start | bytes 24580
Sparse Core Ops, SparseCore 0:
  93.4 90.2 reduce-scatter.2
  185.5 79.3 all-gather.2
  267.5 165.4 all-reduce.3
  435.6 117.5 all-gather.4
  567.7 209.8 reduce-scatter.4
where the time goes:
time: 869 us; the launch traced here: 868 us
  waiting for transfers between devices  582 us (67%)
  blocking collectives  205 us (24%)
  matrix products  30.4 us (3%)
  local copies, waits for them, and re-layouts  18.2 us (2%)
  between operations  17.4 us (2%)
  other arithmetic  14.8 us (2%)
    reduce_scatter x1, waiting for transfers between devices, body(): lax.psum_scatter(lax.dot_general(columns, scaled_err, (((0,), (0,)), ((),...  210 us
    psum x1, waiting for transfers between devices, body(): lax.psum(partial_value.astype(jnp.bfloat16), 'tp').astype(jnp.float32)  168 us
    all_gather x1, waiting for transfers between devices, body(): lax.all_gather(draft_weight, 'req', axis=0, tiled=True)  104 us
    psum x1, blocking collectives, body(): lax.psum((jnp.sum(gradient * gradient), jnp.sum(weights * pred_error * pr...  76.2 us
    all_gather x1, waiting for transfers between devices, body(): full_residual = lax.all_gather(residual, 'tp', axis=2, tiled=True)  75.2 us
    pmax x1, blocking collectives, body(): row_top = lax.pmax(local_top, 'tp')  67.8 us
    unnamed x1, blocking collectives  61 us
    reduce_scatter x1, waiting for transfers between devices, body(): lax.psum_scatter(weighted, 'tp', scatter_dimension=1, tiled=True)  23.9 us
  transfers between devices with their start and end apart: 5, of which 5 were waited for; matrix products, arithmetic and copies ran while one was open for 3% of the time, Pallas kernels for 0%

commit v1 on v0

--- a/solution.py
+++ b/solution.py
@@ -1,8 +1,10 @@
+import functools
 import math
 import jax
 import jax.numpy as jnp
 from jax import lax
 from jax.sharding import PartitionSpec as P
+from jax.lax import all_gather
 
 HEADS = 32
 KV_HEADS = 4
@@ -16,6 +18,13 @@
 CORRECT_ONE = 1.0 - 0.9**10
 CORRECT_TWO = 1.0 - 0.95**10
 LEARN_RATE = 0.001
+
+
+def rates_enter(mine_x, along_axis):
+    return all_gather(mine_x, along_axis).sum(axis=0)
+
+
+divide_streams = functools.partial(rates_enter, along_axis="tp")
 
 
 def closure(parents):
@@ -111,7 +120,7 @@
     partial_value = lax.optimization_barrier(partial_value.astype(jnp.bfloat16)).astype(jnp.float32)
     model_width = partial_value.shape[1]
     block_width = model_width // lax.axis_size("tp")
-    summed = lax.psum(partial_value.astype(jnp.bfloat16), "tp").astype(jnp.float32)
+    summed = divide_streams(partial_value.astype(jnp.bfloat16)).astype(jnp.float32)
     mixed = full_residual.reshape(row_count, model_width).astype(jnp.float32) + summed
     mean_sq = jnp.mean(mixed * mixed, axis=1, keepdims=True)
     features = (mixed * lax.rsqrt(mean_sq + NORM_EPSILON) * norm_gain[None, :]).astype(jnp.bfloat16)

time: 869 us -> 1050 us (1.21)
  waiting for transfers between devices: 582 us -> 734 us
  other arithmetic: 14.8 us -> 36.2 us
    all_gather x0 -> x1, waiting for transfers between devices: none -> 362 us  [rates_enter(): return all_gather(mine_x, along_axis).sum(axis=0)]
    psum x1 -> x0, waiting for transfers between devices: 168 us -> none  [body(): lax.psum(partial_value.astype(jnp.bfloat16), 'tp').astype(jnp.float32)]
    all_gather x1, waiting for transfers between devices: 104 us -> 71 us  [body(): lax.all_gather(draft_weight, 'req', axis=0, tiled=True)]
    reduce_sum x0 -> x1, other arithmetic: none -> 12.9 us  [rates_enter(): return all_gather(mine_x, along_axis).sum(axis=0)]
  transfers between devices with their start and end apart: 5 -> 5, of which waited for: 5 -> 5; matrix products, arithmetic and copies ran while one was open for 3% -> 5% of each run, Pallas kernels for 0% -> 0%
where the time goes in v1:
time: 1050 us; the launch traced here: 1040 us
  waiting for transfers between devices  734 us (70%)
  blocking collectives  205 us (20%)
  other arithmetic  36.2 us (3%)
  matrix products  28.9 us (3%)
  local copies, waits for them, and re-layouts  22.5 us (2%)
  between operations  17.4 us (2%)
    all_gather x1, waiting for transfers between devices, rates_enter(): return all_gather(mine_x, along_axis).sum(axis=0)  362 us
    reduce_scatter x1, waiting for transfers between devices, body(): lax.psum_scatter(lax.dot_general(columns, scaled_err, (((0,), (0,)), ((),...  210 us
    psum x1, blocking collectives, body(): lax.psum((jnp.sum(gradient * gradient), jnp.sum(weights * pred_error * pr...  76.2 us
    all_gather x1, waiting for transfers between devices, body(): lax.all_gather(draft_weight, 'req', axis=0, tiled=True)  71 us
    pmax x1, blocking collectives, body(): row_top = lax.pmax(local_top, 'tp')  67.8 us
    all_gather x1, waiting for transfers between devices, body(): full_residual = lax.all_gather(residual, 'tp', axis=2, tiled=True)  66.7 us
    unnamed x1, blocking collectives  60.9 us
    reduce_scatter x1, waiting for transfers between devices, body(): lax.psum_scatter(weighted, 'tp', scatter_dimension=1, tiled=True)  24.2 us
  transfers between devices with their start and end apart: 5, of which 5 were waited for; matrix products, arithmetic and copies ran while one was open for 5% of the time, Pallas kernels for 0%

profile of v1, /device:TPU:1, one launch (start us, length us, event | category | flops | bytes accessed | tf_op | source)
XLA Modules:
  0.0 1044.6 jit_solution(10009738151687288507)
XLA Ops:
  7.3 1.1 convolution_minimum_fusion.4
  10.3 1.4 copy.102
  12.2 1.5 fusion.41
  13.7 2.9 bitcast_reduce_fusion
  16.6 67.8 %pmax.7 = f32[4,4,8,32]{3,2,1,0:T(8,128)S(1)} all-reduce(f32[4,4,8,32]{3,2,1,0:T(8,128)S(1)} %max.5), channel_id=1, replica_groups=mesh['req'=16,'tp'=16] {'tp'}, use_global_device_ids=true, to_apply=%region_2.3 | all-reduce | flops 4096 | bytes 32768 | tf_op jit(solution)/shard_map/pmax | solution.py:87
  84.9 2.9 fusion.6
  88.4 1.2 copy.85
  89.6 1.5 reshape.132
  91.2 0.8 copy.60
  92.1 3.1 convert_reduce_fusion
  95.4 0.6 dynamic-slice
  96.6 60.9 %all-reduce = f32[128,32]{0,1:T(8,128)S(1)} all-reduce(f32[128,32]{0,1:T(8,128)S(1)} %reshape.133), channel_id=4, replica_groups=mesh['req'=16,'tp'=16] {'tp'}, use_global_device_ids=true, to_apply=%region_6.7.clone | all-reduce | flops 4096 | bytes 32768
  157.7 24.2 %reduce-scatter.3.cloned.1.call-done = f32[128,256]{1,0:T(8,128)} async-done(((f32[128,4096]{1,0:T(8,128)}), f32[128,256]{1,0:T(8,128)}) %reduce-scatter.3.cloned.1.call-update) | async-done | bytes 131088 | tf_op jit(solution)/shard_map/reduce_scatter | solution.py:108
  182.1 4.3 convolution_convert_fusion
  187.9 66.7 %all-gather.5.cloned.1.call-done = bf16[4,32,8192]{2,0,1:T(4,128)(2,1)} async-done(((bf16[4,32,512]{2,0,1:T(4,128)(2,1)}), bf16[4,32,8192]{2,0,1:T(4,128)(2,1)}) %all-gather.5.cloned.1.call-update) | async-done | bytes 2097168 | tf_op jit(solution)/shard_map/all_gather | solution.py:60
  254.7 4.7 copy.61
  259.4 361.9 %all-gather.9.cloned.1.call-done = bf16[2048,8192]{1,0:T(8,128)(2,1)} async-done(((bf16[128,8192]{1,0:T(8,128)(2,1)}), bf16[2048,8192]{1,0:T(8,128)(2,1)}) %all-gather.9.cloned.1.call-update) | async-done | bytes 33554448 | tf_op jit(solution)/shard_map/all_gather | solution.py:24
  621.3 12.9 %reduce_sum.59 = bf16[128,8192]{1,0:T(8,128)(2,1)} reduce(bf16[16,128,8192]{2,1,0:T(8,128)(2,1)} %bitcast.71, bf16[]{:T(256)} %constant.16.clone.1), dimensions={0}, to_apply=%region_7.8 | reduce | flops 15728640 | bytes 35651584 | tf_op jit(solution)/shard_map/reduce_sum | solution.py:24
  634.3 2.3 convert_element_type.85
  636.5 1.9 copy-done.2
  638.5 2.9 multiply_reduce_fusion
  641.6 6.3 multiply_convert_fusion
  647.9 1.4 pad_maximum_fusion
  649.3 8.2 gather_fusion
  657.5 1.1 fusion.16
  658.6 71.0 %all-gather.7.cloned.1.call-done = bf16[8192,512]{1,0:T(8,128)(2,1)} async-done(((bf16[512,512]{1,0:T(8,128)(2,1)}), bf16[8192,512]{1,0:T(8,128)(2,1)}) %all-gather.7.cloned.1.call-update) | async-done | bytes 8388624 | tf_op jit(solution)/shard_map/all_gather | solution.py:143
  729.6 6.0 fusion.13
  735.6 8.2 fusion.12
  743.8 210.0 %reduce-scatter.5.cloned.1.call-done = f32[512,512]{1,0:T(8,128)} async-done(((f32[8192,512]{1,0:T(8,128)}), f32[512,512]{1,0:T(8,128)}) %reduce-scatter.5.cloned.1.call-update) | async-done | bytes 1048592 | tf_op jit(solution)/shard_map/reduce_scatter | solution.py:149
  953.8 2.1 multiply_reduce_fusion.1
  955.9 76.2 %all-reduce.1 = (f32[]{:T(128)}, f32[]{:T(128)}) all-reduce(f32[]{:T(128)} %multiply_reduce_fusion.1, f32[]{:T(128)} %get-tuple-element.16), channel_id=1, replica_groups=mesh['req'=16,'tp'=16] {'req','tp'}, use_global_device_ids=true, to_apply=%region_11.12 | all-reduce | flops 2 | bytes 16 | tf_op jit(solution)/shard_map/psum | solution.py:157
  1033.5 3.4 subtract_convert_fusion
  (87 shorter events, 5.7 us)
Async XLA Ops:
  7.2 80.7 %copy-start = (bf16[4,2,512]{2,1,0:T(2,128)(2,1)S(1)}, bf16[4,2,512]{2,1,0:T(2,128)(2,1)}, u32[]{:S(2)}) copy-start(bf16[4,2,512]{2,1,0:T(2,128)(2,1)} %param.19) | copy-start | bytes 24580
  7.2 4.6 copy-start.8
  7.2 4.9 copy-start.15
  7.2 5.0 copy-start.16
  7.2 174.6 %reduce-scatter.3.cloned.1.call-start = ((), (), s32[]{:S(2)}) async-start(), calls=%async_computation.3 | async-start | bytes 2228224 | tf_op jit(solution)/shard_map/reduce_scatter | solution.py:108
  12.2 72.2 %copy-start.9 = (bf16[4,256,512]{2,1,0:T(8,128)(2,1)S(1)}, bf16[4,256,512]{2,1,0:T(8,128)(2,1)}, u32[]{:S(2)}) copy-start(bf16[4,256,512]{2,1,0:T(8,128)(2,1)} %param.17) | copy-start | bytes 3145732
  89.6 1.6 copy-start.11
  91.1 4.2 copy-start.18
  91.2 163.5 %all-gather.5.cloned.1.call-start = ((), (), s32[]{:S(2)}) async-start(), calls=%async_computation.2 | async-start | bytes 2228224 | tf_op jit(solution)/shard_map/all_gather | solution.py:60
  92.0 529.3 %all-gather.9.cloned.1.call-start = ((), (), s32[]{:S(2)}) async-start(), calls=%async_computation.6 | async-start | bytes 35651584 | tf_op jit(solution)/shard_map/all_gather | solution.py:24
  182.1 5.2 copy-start.14
  182.1 5.3 copy-start.17
  182.1 5.8 copy-start.13
  186.4 543.2 %all-gather.7.cloned.1.call-start = ((), (), s32[]{:S(2)}) async-start(), calls=%async_computation.4 | async-start | bytes 8912896 | tf_op jit(solution)/shard_map/all_gather | solution.py:143
  187.0 766.8 %reduce-scatter.5.cloned.1.call-start = ((), (), s32[]{:S(2)}) async-start(), calls=%async_computation.5 | async-start | bytes 17825792 | tf_op jit(solution)/shard_map/reduce_scatter | solution.py:149
  634.3 4.2 copy-start.3
  636.5 1.9 copy-start.2
  641.6 6.3 copy-start.12
  658.6 77.0 %copy-start.10 = (bf16[128,512]{1,0:T(8,128)(2,1)}, bf16[128,512]{1,0:T(8,128)(2,1)S(1)}, u32[]{:S(2)}) copy-start(bf16[128,512]{1,0:T(8,128)(2,1)S(1)} %fusion.16) | copy-start | bytes 393220
  658.6 77.0 %copy-start.4 = (bf16[128,8192]{1,0:T(8,128)(2,1)S(1)}, bf16[128,8192]{1,0:T(8,128)(2,1)}, u32[]{:S(2)}) copy-start(bf16[128,8192]{1,0:T(8,128)(2,1)} %gather_fusion) | copy-start | bytes 6291460
  743.8 289.7 %copy-start.5 = (bf16[512,512]{1,0:T(8,128)(2,1)S(1)}, bf16[512,512]{1,0:T(8,128)(2,1)}, u32[]{:S(2)}) copy-start(bf16[512,512]{1,0:T(8,128)(2,1)} %param.27) | copy-start | bytes 1572868
  743.8 289.8 %copy-start.6 = (f32[512,512]{1,0:T(8,128)S(1)}, f32[512,512]{1,0:T(8,128)}, u32[]{:S(2)}) copy-start(f32[512,512]{1,0:T(8,128)} %param.28) | copy-start | bytes 3145732
  743.8 289.8 %copy-start.7 = (f32[512,512]{1,0:T(8,128)S(1)}, f32[512,512]{1,0:T(8,128)}, u32[]{:S(2)}) copy-start(f32[512,512]{1,0:T(8,128)} %param.29) | copy-start | bytes 3145732
  743.8 293.1 %copy-start.1 = (bf16[4,2,512]{2,1,0:T(2,128)(2,1)S(1)}, bf16[4,2,512]{2,1,0:T(2,128)(2,1)}, u32[]{:S(2)}) copy-start(bf16[4,2,512]{2,1,0:T(2,128)(2,1)} %param.19) | copy-start | bytes 24580
Sparse Core Ops, SparseCore 0:
  91.3 90.5 reduce-scatter.2
  184.2 70.4 all-gather.4
  256.4 364.8 all-gather.8
  623.9 105.6 all-gather.6
  743.9 209.8 reduce-scatter.4
